TPU v7x, 32 devices: a whole 2x2x4 slice. The times are simulated.
32 devices in a mesh: pipe: 2 (over y), ctx: 16 (over z, x, core).
Axes of the slice: x: 2, y: 2, z: 4, core: 2. Of those that a mesh axis runs over, the one named last changes fastest.
Arguments:
- saved_qkv: bfloat16 [2, 3, 2048, 2048], P('pipe', None, 'ctx'), may hold values from -6 to 6
- handed: bfloat16 [2, 2048, 2048], P('pipe', 'ctx'), may hold values from -6 to 6
- long_filter: bfloat16 [2, 128, 128], P('pipe'), may hold values from -0.5 to 0.5
- short_filter: bfloat16 [2, 3, 3, 2048], P('pipe'), may hold values from -3.5 to 3.5
- doc_lengths: int32 [16], replicated, may hold values from 1 to 512, 2048 in all
Outputs:
- grad_pre: bfloat16 [2, 3, 2048, 2048], P('pipe', None, 'ctx')
- filter_grad: float32 [2, 128, 128], P('pipe')
Inputs may be any that keep to these rules, and one draw needn't show every extreme that they name: `doc_lengths`: documents lie end to end and sum to 2048 tokens; the longest has exactly 512 tokens.
All inputs are finite; a program needn't handle non-finite values.
Results may differ from a plain program's by a relative error of at most 0.0058.
Values may be sent and summed in bfloat16 or wider, within the bound.
A program may use at most 64 MiB of HBM per device.

v0:
```python
import math

import jax
import jax.numpy as jnp
from jax import lax
from jax.sharding import PartitionSpec as P


def from_behind(shard, axis, by):
    count = lax.axis_size(axis)
    return lax.ppermute(shard, axis, [(i, (i + by) % count) for i in range(count)])


def shifted_2(block, axis, distance):
    devices = range(lax.axis_size(axis))
    route = [(i - distance, i) for i in devices if i - distance in devices]
    return lax.ppermute(block, axis, route)


def back_conv(grad_rows, grad_pos, filt, out_len, members, unroll):
    tap_count = filt.shape[0]
    channels = grad_rows.shape[1]

    def step(total, base):
        for offset in range(unroll):
            lag = base * unroll + offset
            ahead = lax.dynamic_slice_in_dim(grad_rows, lag, out_len, 0).astype(jnp.float32)
            ahead_pos = lax.dynamic_slice_in_dim(grad_pos, lag, out_len, 0)
            weights = jnp.repeat(filt[lag].astype(jnp.float32), members)
            total = total + jnp.where((lag <= ahead_pos)[:, None], ahead * weights[None, :], 0.0)
        return (total, None)

    bases = jnp.arange(tap_count // unroll, dtype=jnp.int32)
    result, _ = lax.scan(step, jnp.zeros((out_len, channels), jnp.float32), bases)
    return result


def body(saved_qkv, handed, long_filter, short_filter, doc_lengths):
    query_rows = saved_qkv[0, 0]
    key_rows = saved_qkv[0, 1]
    value_rows = saved_qkv[0, 2]
    filt = long_filter[0]
    tap_count, groups = filt.shape
    row_count, channels = query_rows.shape
    members = channels // groups
    short_taps = short_filter.shape[2]
    unroll = math.gcd(tap_count, 16)
    devices = lax.axis_size("ctx")
    device_index = lax.axis_index("ctx")
    starts = jnp.cumsum(doc_lengths) - doc_lengths
    global_rows = device_index * row_count + jnp.arange(row_count + tap_count, dtype=jnp.int32)
    latest = jnp.max(jnp.where(starts[None, :] <= global_rows[:, None], starts[None, :], 0), axis=1)
    position = global_rows - latest
    own_pos = position[:row_count]
    incoming = from_behind(handed[0], "pipe", -1)
    product = (key_rows.astype(jnp.float32) * value_rows.astype(jnp.float32)).astype(jnp.bfloat16)
    tail_rows = shifted_2(product, "ctx", 1)
    extended = jnp.concatenate([tail_rows, product], axis=0)
    conv_grad = (incoming.astype(jnp.float32) * query_rows.astype(jnp.float32)).astype(jnp.bfloat16)
    grad_wide = conv_grad.astype(jnp.float32)

    def forward_step(total, base):
        columns = []
        for offset in range(unroll):
            lag = base * unroll + offset
            shifted = lax.dynamic_slice_in_dim(extended, tap_count - lag, row_count, 0).astype(
                jnp.float32
            )
            weights = jnp.repeat(filt[lag].astype(jnp.float32), members)
            usable = (lag <= own_pos)[:, None]
            total = total + jnp.where(usable, shifted * weights[None, :], 0.0)
            pair = jnp.sum(
                (grad_wide * shifted).reshape(row_count, groups, members), axis=2
            ).astype(jnp.bfloat16)
            pair = lax.optimization_barrier(pair).astype(jnp.float32)
            columns.append(jnp.sum(jnp.where(usable, pair, 0.0), axis=0))
        return (total, jnp.stack(columns))

    bases = jnp.arange(tap_count // unroll, dtype=jnp.int32)
    conv_out, filter_cols = lax.scan(
        forward_step, jnp.zeros((row_count, channels), jnp.float32), bases
    )
    filter_sum = filter_cols.reshape(tap_count, groups)
    head_rows = shifted_2(conv_grad, "ctx", -1)
    joined = jnp.concatenate([conv_grad, head_rows], axis=0)
    own_grad = back_conv(joined, position, filt, row_count, members, unroll)
    query_grad = (incoming.astype(jnp.float32) * conv_out).astype(jnp.bfloat16)
    key_grad = (own_grad * value_rows.astype(jnp.float32)).astype(jnp.bfloat16)
    value_grad = (own_grad * key_rows.astype(jnp.float32)).astype(jnp.bfloat16)
    stacked = jnp.stack([query_grad, key_grad, value_grad])
    rim_rows = shifted_2(stacked[:, : short_taps - 1], "ctx", -1)
    stacked_ext = jnp.concatenate([stacked, rim_rows], axis=1)
    weights_all = short_filter[0]
    total = jnp.zeros((3, row_count, channels), jnp.float32)
    for shift_by in range(short_taps):
        usable = (shift_by <= position[shift_by : shift_by + row_count])[None, :, None]
        weights = weights_all[:, shift_by].astype(jnp.float32)[:, None, :]
        total = total + jnp.where(
            usable,
            weights * stacked_ext[:, shift_by : shift_by + row_count].astype(jnp.float32),
            0.0,
        )
    grad_pre = total.astype(jnp.bfloat16)[None]
    summed = lax.psum(filter_sum, "ctx")
    filter_grad = (summed / math.sqrt(row_count * devices * members))[None]
    return (grad_pre, filter_grad)


def solution(mesh):
    return jax.shard_map(
        body,
        mesh=mesh,
        in_specs=(
            P("pipe", None, "ctx", None),
            P("pipe", "ctx", None),
            P("pipe", None, None),
            P("pipe", None, None, None),
            P(),
        ),
        out_specs=(P("pipe", None, "ctx", None), P("pipe", None, None)),
        check_vma=False,
    )
```

profile of v0, /device:TPU:1, one launch (start us, length us, event | category | flops | bytes accessed | tf_op | source)
XLA Modules:
  0.0 409.2 jit_solution(385893030262521515)
XLA Ops:
  9.3 11.8 %collective-permute-done = bf16[128,2048]{1,0:T(8,128)(2,1)S(1)} collective-permute-done((bf16[128,2048]{1,0:T(8,128)(2,1)}, bf16[128,2048]{1,0:T(8,128)(2,1)S(1)}, u32[]{:S(2)}, u32[]{:S(2)}) %collective-permute-start) | collective-permute-done | bytes 524320 | tf_op jit(solution)/shard_map/ppermute | solution.py:11
  22.6 3.2 collective-permute-start.2
  27.5 6.5 %collective-permute-done.2 = bf16[128,2048]{1,0:T(8,128)(2,1)S(1)} collective-permute-done((bf16[128,2048]{1,0:T(8,128)(2,1)S(1)}, bf16[128,2048]{1,0:T(8,128)(2,1)S(1)}, u32[]{:S(2)}, u32[]{:S(2)}) %collective-permute-start.2) | collective-permute-done | bytes 524320 | tf_op jit(solution)/shard_map/ppermute | solution.py:17
  34.1 81.4 %while.30 = (s32[]{:T(128)}, f32[128,2048]{1,0:T(8,128)S(1)}, s32[8]{0:T(128)S(1)}, s32[256]{0:T(256)S(1)}, bf16[256,2048]{1,0:T(8,128)(2,1)S(1)}, /*index=5*/bf...) while((s32[]{:T(128)}, f32[128,2048]{1,0:T(8,128)S(1)}, ...), condition=%wide.region_37.38_spmd.clone, body=%wide.region_36.37_spmd.clone.sunk | while | flops 17043556 | bytes 11044691 | solution.py:34
  38.6 5.6 %fusion.128 = f32[128,2048]{1,0:T(8,128)S(1)} fusion(f32[128,2048]{1,0:T(8,128)S(1)} %get-tuple-element.835, f32[2048]{0:T(1024)S(1)} %mul.1435, bf16[256,2048]{1,0:T(8,128)(2,1)S(1)} %get-tuple-element.893, s32[]{:T(128)S(6)} %select_n.1196, f32[2048]{0:T(1024)S(1)} %mul.1436, s32[]{:T(128)S(6)} %select_n.1197, f32[2048]{0:T(1024)S(1)} %mul.1437, ...), kind=kLoop, calls=%fused_computation.176.clone.1 | loop fusion | flops 17039360 | bytes 10618945 | tf_op jit(solution)/shard_map/while/body/eval_jaxpr/add | solution.py:30
  48.8 5.6 %fusion.128 = f32[128,2048]{1,0:T(8,128)S(1)} fusion(f32[128,2048]{1,0:T(8,128)S(1)} %get-tuple-element.835, f32[2048]{0:T(1024)S(1)} %mul.1435, bf16[256,2048]{1,0:T(8,128)(2,1)S(1)} %get-tuple-element.893, s32[]{:T(128)S(6)} %select_n.1196, f32[2048]{0:T(1024)S(1)} %mul.1436, s32[]{:T(128)S(6)} %select_n.1197, f32[2048]{0:T(1024)S(1)} %mul.1437, ...), kind=kLoop, calls=%fused_computation.176.clone.1 | loop fusion | flops 17039360 | bytes 10618945 | tf_op jit(solution)/shard_map/while/body/eval_jaxpr/add | solution.py:30
  59.0 5.6 %fusion.128 = f32[128,2048]{1,0:T(8,128)S(1)} fusion(f32[128,2048]{1,0:T(8,128)S(1)} %get-tuple-element.835, f32[2048]{0:T(1024)S(1)} %mul.1435, bf16[256,2048]{1,0:T(8,128)(2,1)S(1)} %get-tuple-element.893, s32[]{:T(128)S(6)} %select_n.1196, f32[2048]{0:T(1024)S(1)} %mul.1436, s32[]{:T(128)S(6)} %select_n.1197, f32[2048]{0:T(1024)S(1)} %mul.1437, ...), kind=kLoop, calls=%fused_computation.176.clone.1 | loop fusion | flops 17039360 | bytes 10618945 | tf_op jit(solution)/shard_map/while/body/eval_jaxpr/add | solution.py:30
  69.2 5.6 %fusion.128 = f32[128,2048]{1,0:T(8,128)S(1)} fusion(f32[128,2048]{1,0:T(8,128)S(1)} %get-tuple-element.835, f32[2048]{0:T(1024)S(1)} %mul.1435, bf16[256,2048]{1,0:T(8,128)(2,1)S(1)} %get-tuple-element.893, s32[]{:T(128)S(6)} %select_n.1196, f32[2048]{0:T(1024)S(1)} %mul.1436, s32[]{:T(128)S(6)} %select_n.1197, f32[2048]{0:T(1024)S(1)} %mul.1437, ...), kind=kLoop, calls=%fused_computation.176.clone.1 | loop fusion | flops 17039360 | bytes 10618945 | tf_op jit(solution)/shard_map/while/body/eval_jaxpr/add | solution.py:30
  79.3 5.6 %fusion.128 = f32[128,2048]{1,0:T(8,128)S(1)} fusion(f32[128,2048]{1,0:T(8,128)S(1)} %get-tuple-element.835, f32[2048]{0:T(1024)S(1)} %mul.1435, bf16[256,2048]{1,0:T(8,128)(2,1)S(1)} %get-tuple-element.893, s32[]{:T(128)S(6)} %select_n.1196, f32[2048]{0:T(1024)S(1)} %mul.1436, s32[]{:T(128)S(6)} %select_n.1197, f32[2048]{0:T(1024)S(1)} %mul.1437, ...), kind=kLoop, calls=%fused_computation.176.clone.1 | loop fusion | flops 17039360 | bytes 10618945 | tf_op jit(solution)/shard_map/while/body/eval_jaxpr/add | solution.py:30
  89.5 5.6 %fusion.128 = f32[128,2048]{1,0:T(8,128)S(1)} fusion(f32[128,2048]{1,0:T(8,128)S(1)} %get-tuple-element.835, f32[2048]{0:T(1024)S(1)} %mul.1435, bf16[256,2048]{1,0:T(8,128)(2,1)S(1)} %get-tuple-element.893, s32[]{:T(128)S(6)} %select_n.1196, f32[2048]{0:T(1024)S(1)} %mul.1436, s32[]{:T(128)S(6)} %select_n.1197, f32[2048]{0:T(1024)S(1)} %mul.1437, ...), kind=kLoop, calls=%fused_computation.176.clone.1 | loop fusion | flops 17039360 | bytes 10618945 | tf_op jit(solution)/shard_map/while/body/eval_jaxpr/add | solution.py:30
  99.7 5.6 %fusion.128 = f32[128,2048]{1,0:T(8,128)S(1)} fusion(f32[128,2048]{1,0:T(8,128)S(1)} %get-tuple-element.835, f32[2048]{0:T(1024)S(1)} %mul.1435, bf16[256,2048]{1,0:T(8,128)(2,1)S(1)} %get-tuple-element.893, s32[]{:T(128)S(6)} %select_n.1196, f32[2048]{0:T(1024)S(1)} %mul.1436, s32[]{:T(128)S(6)} %select_n.1197, f32[2048]{0:T(1024)S(1)} %mul.1437, ...), kind=kLoop, calls=%fused_computation.176.clone.1 | loop fusion | flops 17039360 | bytes 10618945 | tf_op jit(solution)/shard_map/while/body/eval_jaxpr/add | solution.py:30
  109.8 5.6 %fusion.128 = f32[128,2048]{1,0:T(8,128)S(1)} fusion(f32[128,2048]{1,0:T(8,128)S(1)} %get-tuple-element.835, f32[2048]{0:T(1024)S(1)} %mul.1435, bf16[256,2048]{1,0:T(8,128)(2,1)S(1)} %get-tuple-element.893, s32[]{:T(128)S(6)} %select_n.1196, f32[2048]{0:T(1024)S(1)} %mul.1436, s32[]{:T(128)S(6)} %select_n.1197, f32[2048]{0:T(1024)S(1)} %mul.1437, ...), kind=kLoop, calls=%fused_computation.176.clone.1 | loop fusion | flops 17039360 | bytes 10618945 | tf_op jit(solution)/shard_map/while/body/eval_jaxpr/add | solution.py:30
  120.5 5.6 %collective-permute-done.1 = bf16[128,2048]{1,0:T(8,128)(2,1)} collective-permute-done((bf16[128,2048]{1,0:T(8,128)(2,1)S(1)}, bf16[128,2048]{1,0:T(8,128)(2,1)}, u32[]{:S(2)}, u32[]{:S(2)}) %collective-permute-start.1) | collective-permute-done | bytes 524320 | tf_op jit(solution)/shard_map/ppermute | solution.py:17
  129.7 178.6 %while.29 = (s32[]{:T(128)}, f32[128,2048]{0,1:T(8,128)S(1)}, f32[8,16,128]{2,1,0:T(8,128)}, s32[8]{0:T(128)S(1)}, s32[128]{0:T(128)S(1)}, /*index=5*/bf16[256,2...) while((s32[]{:T(128)}, f32[128,2048]{0,1:T(8,128)S(1)}, ...), condition=%wide.region_35.36_spmd.clone, body=%wide.region_2.35_spmd.clone.sunk | while | flops 30148740 | bytes 21566524 | solution.py:80
  131.1 6.9 %bitcast_reduce_fusion.17 = (bf16[128,128]{0,1:T(8,128)(2,1)S(1)}, bf16[128,128]{0,1:T(8,128)(2,1)S(1)}, bf16[128,128]{0,1:T(8,128)(2,1)S(1)}, bf16[128,128]{0,1...) fusion(f32[128,2048]{0,1:T(8,128)S(1)} %get-tuple-element.1035,, ...), kind=kLoop, calls=%fused_computation.64.clone.1 | loop fusion | flops 12320768 | bytes 9961536 | tf_op jit(solution)/shard_map/while/body/eval_jaxpr/reduce_sum | solution.py:72
  142.5 9.6 %fusion.126 = f32[128,2048]{0,1:T(8,128)S(1)} fusion(f32[128,2048]{0,1:T(8,128)S(1)} %get-tuple-element.987, f32[2048]{0:T(1024)S(1)} %mul.1386, f32[2048]{0:T(1024)S(1)} %mul.1387, f32[2048]{0:T(1024)S(1)} %mul.1388, f32[2048]{0:T(1024)S(1)} %mul.1389, f32[2048]{0:T(1024)S(1)} %mul.1390, f32[2048]{0:T(1024)S(1)} %mul.1391, f32[2048]{0:T(1024)S(1)} %mul.1392, ...), kind=kLoop, calls=%fused_computation.48.clone.1 | loop fusion | flops 17039360 | bytes 10618945 | tf_op jit(solution)/shard_map/while/body/eval_jaxpr/add | solution.py:71
  153.4 6.9 %bitcast_reduce_fusion.17 = (bf16[128,128]{0,1:T(8,128)(2,1)S(1)}, bf16[128,128]{0,1:T(8,128)(2,1)S(1)}, bf16[128,128]{0,1:T(8,128)(2,1)S(1)}, bf16[128,128]{0,1...) fusion(f32[128,2048]{0,1:T(8,128)S(1)} %get-tuple-element.1035,, ...), kind=kLoop, calls=%fused_computation.64.clone.1 | loop fusion | flops 12320768 | bytes 9961536 | tf_op jit(solution)/shard_map/while/body/eval_jaxpr/reduce_sum | solution.py:72
  164.8 9.6 %fusion.126 = f32[128,2048]{0,1:T(8,128)S(1)} fusion(f32[128,2048]{0,1:T(8,128)S(1)} %get-tuple-element.987, f32[2048]{0:T(1024)S(1)} %mul.1386, f32[2048]{0:T(1024)S(1)} %mul.1387, f32[2048]{0:T(1024)S(1)} %mul.1388, f32[2048]{0:T(1024)S(1)} %mul.1389, f32[2048]{0:T(1024)S(1)} %mul.1390, f32[2048]{0:T(1024)S(1)} %mul.1391, f32[2048]{0:T(1024)S(1)} %mul.1392, ...), kind=kLoop, calls=%fused_computation.48.clone.1 | loop fusion | flops 17039360 | bytes 10618945 | tf_op jit(solution)/shard_map/while/body/eval_jaxpr/add | solution.py:71
  175.8 6.9 %bitcast_reduce_fusion.17 = (bf16[128,128]{0,1:T(8,128)(2,1)S(1)}, bf16[128,128]{0,1:T(8,128)(2,1)S(1)}, bf16[128,128]{0,1:T(8,128)(2,1)S(1)}, bf16[128,128]{0,1...) fusion(f32[128,2048]{0,1:T(8,128)S(1)} %get-tuple-element.1035,, ...), kind=kLoop, calls=%fused_computation.64.clone.1 | loop fusion | flops 12320768 | bytes 9961536 | tf_op jit(solution)/shard_map/while/body/eval_jaxpr/reduce_sum | solution.py:72
  187.1 9.6 %fusion.126 = f32[128,2048]{0,1:T(8,128)S(1)} fusion(f32[128,2048]{0,1:T(8,128)S(1)} %get-tuple-element.987, f32[2048]{0:T(1024)S(1)} %mul.1386, f32[2048]{0:T(1024)S(1)} %mul.1387, f32[2048]{0:T(1024)S(1)} %mul.1388, f32[2048]{0:T(1024)S(1)} %mul.1389, f32[2048]{0:T(1024)S(1)} %mul.1390, f32[2048]{0:T(1024)S(1)} %mul.1391, f32[2048]{0:T(1024)S(1)} %mul.1392, ...), kind=kLoop, calls=%fused_computation.48.clone.1 | loop fusion | flops 17039360 | bytes 10618945 | tf_op jit(solution)/shard_map/while/body/eval_jaxpr/add | solution.py:71
  198.1 6.9 %bitcast_reduce_fusion.17 = (bf16[128,128]{0,1:T(8,128)(2,1)S(1)}, bf16[128,128]{0,1:T(8,128)(2,1)S(1)}, bf16[128,128]{0,1:T(8,128)(2,1)S(1)}, bf16[128,128]{0,1...) fusion(f32[128,2048]{0,1:T(8,128)S(1)} %get-tuple-element.1035,, ...), kind=kLoop, calls=%fused_computation.64.clone.1 | loop fusion | flops 12320768 | bytes 9961536 | tf_op jit(solution)/shard_map/while/body/eval_jaxpr/reduce_sum | solution.py:72
  209.4 9.6 %fusion.126 = f32[128,2048]{0,1:T(8,128)S(1)} fusion(f32[128,2048]{0,1:T(8,128)S(1)} %get-tuple-element.987, f32[2048]{0:T(1024)S(1)} %mul.1386, f32[2048]{0:T(1024)S(1)} %mul.1387, f32[2048]{0:T(1024)S(1)} %mul.1388, f32[2048]{0:T(1024)S(1)} %mul.1389, f32[2048]{0:T(1024)S(1)} %mul.1390, f32[2048]{0:T(1024)S(1)} %mul.1391, f32[2048]{0:T(1024)S(1)} %mul.1392, ...), kind=kLoop, calls=%fused_computation.48.clone.1 | loop fusion | flops 17039360 | bytes 10618945 | tf_op jit(solution)/shard_map/while/body/eval_jaxpr/add | solution.py:71
  220.4 6.9 %bitcast_reduce_fusion.17 = (bf16[128,128]{0,1:T(8,128)(2,1)S(1)}, bf16[128,128]{0,1:T(8,128)(2,1)S(1)}, bf16[128,128]{0,1:T(8,128)(2,1)S(1)}, bf16[128,128]{0,1...) fusion(f32[128,2048]{0,1:T(8,128)S(1)} %get-tuple-element.1035,, ...), kind=kLoop, calls=%fused_computation.64.clone.1 | loop fusion | flops 12320768 | bytes 9961536 | tf_op jit(solution)/shard_map/while/body/eval_jaxpr/reduce_sum | solution.py:72
  231.8 9.6 %fusion.126 = f32[128,2048]{0,1:T(8,128)S(1)} fusion(f32[128,2048]{0,1:T(8,128)S(1)} %get-tuple-element.987, f32[2048]{0:T(1024)S(1)} %mul.1386, f32[2048]{0:T(1024)S(1)} %mul.1387, f32[2048]{0:T(1024)S(1)} %mul.1388, f32[2048]{0:T(1024)S(1)} %mul.1389, f32[2048]{0:T(1024)S(1)} %mul.1390, f32[2048]{0:T(1024)S(1)} %mul.1391, f32[2048]{0:T(1024)S(1)} %mul.1392, ...), kind=kLoop, calls=%fused_computation.48.clone.1 | loop fusion | flops 17039360 | bytes 10618945 | tf_op jit(solution)/shard_map/while/body/eval_jaxpr/add | solution.py:71
  242.7 6.9 %bitcast_reduce_fusion.17 = (bf16[128,128]{0,1:T(8,128)(2,1)S(1)}, bf16[128,128]{0,1:T(8,128)(2,1)S(1)}, bf16[128,128]{0,1:T(8,128)(2,1)S(1)}, bf16[128,128]{0,1...) fusion(f32[128,2048]{0,1:T(8,128)S(1)} %get-tuple-element.1035,, ...), kind=kLoop, calls=%fused_computation.64.clone.1 | loop fusion | flops 12320768 | bytes 9961536 | tf_op jit(solution)/shard_map/while/body/eval_jaxpr/reduce_sum | solution.py:72
  254.1 9.6 %fusion.126 = f32[128,2048]{0,1:T(8,128)S(1)} fusion(f32[128,2048]{0,1:T(8,128)S(1)} %get-tuple-element.987, f32[2048]{0:T(1024)S(1)} %mul.1386, f32[2048]{0:T(1024)S(1)} %mul.1387, f32[2048]{0:T(1024)S(1)} %mul.1388, f32[2048]{0:T(1024)S(1)} %mul.1389, f32[2048]{0:T(1024)S(1)} %mul.1390, f32[2048]{0:T(1024)S(1)} %mul.1391, f32[2048]{0:T(1024)S(1)} %mul.1392, ...), kind=kLoop, calls=%fused_computation.48.clone.1 | loop fusion | flops 17039360 | bytes 10618945 | tf_op jit(solution)/shard_map/while/body/eval_jaxpr/add | solution.py:71
  265.1 6.9 %bitcast_reduce_fusion.17 = (bf16[128,128]{0,1:T(8,128)(2,1)S(1)}, bf16[128,128]{0,1:T(8,128)(2,1)S(1)}, bf16[128,128]{0,1:T(8,128)(2,1)S(1)}, bf16[128,128]{0,1...) fusion(f32[128,2048]{0,1:T(8,128)S(1)} %get-tuple-element.1035,, ...), kind=kLoop, calls=%fused_computation.64.clone.1 | loop fusion | flops 12320768 | bytes 9961536 | tf_op jit(solution)/shard_map/while/body/eval_jaxpr/reduce_sum | solution.py:72
  276.4 9.6 %fusion.126 = f32[128,2048]{0,1:T(8,128)S(1)} fusion(f32[128,2048]{0,1:T(8,128)S(1)} %get-tuple-element.987, f32[2048]{0:T(1024)S(1)} %mul.1386, f32[2048]{0:T(1024)S(1)} %mul.1387, f32[2048]{0:T(1024)S(1)} %mul.1388, f32[2048]{0:T(1024)S(1)} %mul.1389, f32[2048]{0:T(1024)S(1)} %mul.1390, f32[2048]{0:T(1024)S(1)} %mul.1391, f32[2048]{0:T(1024)S(1)} %mul.1392, ...), kind=kLoop, calls=%fused_computation.48.clone.1 | loop fusion | flops 17039360 | bytes 10618945 | tf_op jit(solution)/shard_map/while/body/eval_jaxpr/add | solution.py:71
  287.4 6.9 %bitcast_reduce_fusion.17 = (bf16[128,128]{0,1:T(8,128)(2,1)S(1)}, bf16[128,128]{0,1:T(8,128)(2,1)S(1)}, bf16[128,128]{0,1:T(8,128)(2,1)S(1)}, bf16[128,128]{0,1...) fusion(f32[128,2048]{0,1:T(8,128)S(1)} %get-tuple-element.1035,, ...), kind=kLoop, calls=%fused_computation.64.clone.1 | loop fusion | flops 12320768 | bytes 9961536 | tf_op jit(solution)/shard_map/while/body/eval_jaxpr/reduce_sum | solution.py:72
  298.7 9.6 %fusion.126 = f32[128,2048]{0,1:T(8,128)S(1)} fusion(f32[128,2048]{0,1:T(8,128)S(1)} %get-tuple-element.987, f32[2048]{0:T(1024)S(1)} %mul.1386, f32[2048]{0:T(1024)S(1)} %mul.1387, f32[2048]{0:T(1024)S(1)} %mul.1388, f32[2048]{0:T(1024)S(1)} %mul.1389, f32[2048]{0:T(1024)S(1)} %mul.1390, f32[2048]{0:T(1024)S(1)} %mul.1391, f32[2048]{0:T(1024)S(1)} %mul.1392, ...), kind=kLoop, calls=%fused_computation.48.clone.1 | loop fusion | flops 17039360 | bytes 10618945 | tf_op jit(solution)/shard_map/while/body/eval_jaxpr/add | solution.py:71
  312.1 3.9 collective-permute-done.3
  318.8 82.1 %all-reduce.2.cloned.1.call-done = f32[128,128]{1,0:T(8,128)} async-done(((f32[128,128]{1,0:T(8,128)}), f32[128,128]{1,0:T(8,128)}) %all-reduce.2.cloned.1.call-update) | async-done | bytes 65552 | tf_op jit(solution)/shard_map/psum | solution.py:104
  (697 shorter events, 90.5 us)
Async XLA Ops:
  7.2 393.7 %all-reduce.2.cloned.1.call-start = ((), (), s32[]{:S(2)}) async-start(), calls=%async_computation | async-start | bytes 131072 | tf_op jit(solution)/shard_map/psum | solution.py:104
  7.2 26.9 %copy-start.5 = (bf16[1,128,128]{2,1,0:T(8,128)(2,1)S(1)}, bf16[1,128,128]{2,1,0:T(8,128)(2,1)}, u32[]{:S(2)}) copy-start(bf16[1,128,128]{2,1,0:T(8,128)(2,1)} %param.11) | copy-start | bytes 98308
  7.2 14.0 %collective-permute-start = (bf16[128,2048]{1,0:T(8,128)(2,1)}, bf16[128,2048]{1,0:T(8,128)(2,1)S(1)}, u32[]{:S(2)}, u32[]{:S(2)}) collective-permute-start(bf16[128,2048]{1,0:T(8,128)(2,1)} %bitcast.309), channel_id=1, source_target_pairs={{0,16},{16,0},{1,17},{17,1},{2,18},{18,2},{3,19},{19,3},{4,20},{20... | collective-permute-start | bytes 1572872 | tf_op jit(solution)/shard_map/ppermute | solution.py:11
  21.2 4.6 %copy-start.4 = (bf16[128,2048]{1,0:T(8,128)(2,1)}, bf16[128,2048]{1,0:T(8,128)(2,1)S(1)}, u32[]{:S(2)}) copy-start(bf16[128,2048]{1,0:T(8,128)(2,1)S(1)} %collective-permute-done) | copy-start | bytes 1572868
  22.6 11.5 %copy-start.2 = (bf16[128,2048]{1,0:T(8,128)(2,1)}, bf16[128,2048]{1,0:T(8,128)(2,1)S(1)}, u32[]{:S(2)}) copy-start(bf16[128,2048]{1,0:T(8,128)(2,1)S(1)} %fusion.112) | copy-start | bytes 1572868
  22.6 11.3 %collective-permute-start.2 = (bf16[128,2048]{1,0:T(8,128)(2,1)S(1)}, bf16[128,2048]{1,0:T(8,128)(2,1)S(1)}, u32[]{:S(2)}, u32[]{:S(2)}) collective-permute-start(bf16[128,2048]{1,0:T(8,128)(2,1)S(1)} %fusion.112), channel_id=1, source_target_pairs={{1,0},{2,1},{3,2},{4,3},{5,4},{6,5},{7,6},{8,7},{9,8},{10,9},{11,1... | collective-permute-start | bytes 1572872 | tf_op jit(solution)/shard_map/ppermute | solution.py:17
  115.5 4.7 %copy-start.6 = (bf16[1,3,3,2048]{3,2,1,0:T(4,128)(2,1)S(1)}, bf16[1,3,3,2048]{3,2,1,0:T(4,128)(2,1)}, u32[]{:S(2)}) copy-start(bf16[1,3,3,2048]{3,2,1,0:T(4,128)(2,1)} %param.12) | copy-start | bytes 110596
  115.5 4.8 %copy-start.3 = (bf16[128,2048]{1,0:T(8,128)(2,1)S(1)}, bf16[128,2048]{1,0:T(8,128)(2,1)}, u32[]{:S(2)}) copy-start(bf16[128,2048]{1,0:T(8,128)(2,1)} %copy-done.2) | copy-start | bytes 1572868
  118.0 8.0 %collective-permute-start.1 = (bf16[128,2048]{1,0:T(8,128)(2,1)S(1)}, bf16[128,2048]{1,0:T(8,128)(2,1)}, u32[]{:S(2)}, u32[]{:S(2)}) collective-permute-start(bf16[128,2048]{1,0:T(8,128)(2,1)S(1)} %get-tuple-element.492), channel_id=1, source_target_pairs={{0,1},{1,2},{2,3},{3,4},{4,5},{5,6},{6,7},{7,8},{8,9},{9,10},{10,1... | collective-permute-start | bytes 1572872 | tf_op jit(solution)/shard_map/ppermute | solution.py:17
  308.3 1.5 copy-start
  308.4 1.5 copy-start.1
  310.1 6.0 %collective-permute-start.3 = (bf16[3,2,2048]{2,1,0:T(2,128)(2,1)S(1)}, bf16[3,2,2048]{2,1,0:T(2,128)(2,1)S(1)}, u32[]{:S(2)}, u32[]{:S(2)}) collective-permute-start(bf16[3,2,2048]{2,1,0:T(2,128)(2,1)S(1)} %slice.51), channel_id=1, source_target_pairs={{1,0},{2,1},{3,2},{4,3},{5,4},{6,5},{7,6},{8,7},{9,8},{10,9},{11,1... | collective-permute-start | bytes 73736 | tf_op jit(solution)/shard_map/ppermute | solution.py:17
Sparse Core Ops, SparseCore 0:
  312.3 88.5 all-reduce.1
where the time goes:
time: 411 us; the launch traced here: 409 us
  other arithmetic  200 us (49%)
  waiting for transfers between devices  110 us (27%)
  local copies, waits for them, and re-layouts  61.2 us (15%)
  between operations  14.3 us (3%)
  loops' own time  14.2 us (3%)
  starting transfers between devices  9.33 us (2%)
    psum x1, waiting for transfers between devices, body(): summed = lax.psum(filter_sum, 'ctx')  82.1 us
    add x8, other arithmetic, forward_step(): total = total + jnp.where(usable, shifted * weights[None, :], 0.0)  76.8 us
    reduce_sum x8, other arithmetic, forward_step(): jnp.sum((grad_wide * shifted).reshape(row_count, groups, members), axis=2)  55.5 us
    add x8, other arithmetic, step(): total + jnp.where((lag <= ahead_pos)[:, None], ahead * weights[None, :],...  44.8 us
    ppermute x3, waiting for transfers between devices, shifted_2(): return lax.ppermute(block, axis, route)  16 us
    mul x128, local copies, waits for them, and re-layouts, forward_step(): total = total + jnp.where(usable, shifted * weights[None, :], 0.0)  12.2 us
    mul x128, local copies, waits for them, and re-layouts, step(): ahead * weights[None, :]  12.2 us
    ppermute x1, waiting for transfers between devices, from_behind(): lax.ppermute(shard, axis, [(i, (i + by) % count) for i in range(count)])  11.8 us
  transfers between devices with their start and end apart: 5, of which 5 were waited for; matrix products, arithmetic and copies ran while one was open for 1% of the time, Pallas kernels for 0%

commit v1 on v0

v1 whole, which is shorter than its diff:
```python
import functools
import math

import jax
import jax.numpy as jnp
from jax import lax
from jax.experimental import pallas as pl
from jax.experimental.pallas import tpu as pltpu
from jax.sharding import PartitionSpec as P

MESH = pl.DeviceIdType.MESH
F32 = jnp.float32
BF16 = jnp.bfloat16
LANES = 128
RIM = 8


def positions(rows, docs_ref):
    latest = jnp.zeros(rows.shape, jnp.int32)
    start = jnp.int32(0)
    for doc in range(docs_ref.shape[0]):
        latest = jnp.maximum(latest, jnp.where(start <= rows, start, 0))
        start = start + docs_ref[doc]
    return rows - latest


def kernel(
    sections, devices, chunks,
    docs_ref, qkv_hbm, handed_hbm, filt_ref, short_ref,
    out_hbm, fg_ref,
    qkv, inc, zz, gg, ysc, dsc, obuf, lhs, lhs3, fdir, frev, shortf,
    m_own, m_prev, t_own, t_next, r_own, r_prev, u_rows,
    acc, part, parts_in, gath,
    in_sem, out_sem, inc_s, inc_r, z_s, z_r, g_s, g_r, rim_s, rim_r, rs_s, rs_r, ag_s, ag_r,
):
    sec = lax.axis_index("pipe")
    me = lax.axis_index("ctx")
    count, channels = inc.shape
    groups = fdir.shape[0]
    members = channels // groups
    per_tile = LANES // members
    wide = channels // chunks
    tiles = wide // LANES
    share = groups // devices
    first, last = me == 0, me == devices - 1
    ahead = lax.rem(sec + sections - 1, sections)
    behind = lax.rem(sec + 1, sections)

    loads = [
        pltpu.make_async_copy(qkv_hbm.at[0, i], qkv.at[i], in_sem.at[i]) for i in range(3)
    ]
    for i in (1, 2, 0):
        loads[i].start()

    barrier = pltpu.get_barrier_semaphore()
    pl.semaphore_signal(barrier, inc=1, device_id={"pipe": behind}, device_id_type=MESH)

    def greet(k, carry):
        peer = lax.rem(me + k, devices)
        pl.semaphore_signal(barrier, inc=1, device_id={"ctx": peer}, device_id_type=MESH)
        return carry

    lax.fori_loop(1, devices, greet, 0)
    pl.semaphore_wait(barrier, devices)

    def cols(c):
        return pl.ds(c * wide, wide)

    def send_inc(c):
        return pltpu.make_async_remote_copy(
            handed_hbm.at[0, :, cols(c)], inc.at[:, cols(c)], inc_s.at[c], inc_r.at[c],
            device_id={"pipe": ahead}, device_id_type=MESH)

    def send_z(c):
        return pltpu.make_async_remote_copy(
            zz.at[pl.ds(0, count), cols(c)], zz.at[pl.ds(count, count), cols(c)],
            z_s.at[c], z_r.at[c],
            device_id={"ctx": lax.rem(me + 1, devices)}, device_id_type=MESH)

    def send_g(c):
        return pltpu.make_async_remote_copy(
            gg.at[pl.ds(0, count), cols(c)], gg.at[pl.ds(count, count), cols(c)],
            g_s.at[c], g_r.at[c],
            device_id={"ctx": lax.rem(me + devices - 1, devices)}, device_id_type=MESH)

    def send_rim(c):
        return pltpu.make_async_remote_copy(
            dsc.at[:, pl.ds(0, RIM), cols(c)], dsc.at[:, pl.ds(count, RIM), cols(c)],
            rim_s.at[c], rim_r.at[c],
            device_id={"ctx": lax.rem(me + devices - 1, devices)}, device_id_type=MESH)

    def send_part(k):
        peer = lax.rem(me + k, devices)
        return pltpu.make_async_remote_copy(
            part.at[peer], parts_in.at[k], rs_s.at[k], rs_r.at[k],
            device_id={"ctx": peer}, device_id_type=MESH)

    def send_sum(k):
        peer = lax.rem(me + k, devices)
        return pltpu.make_async_remote_copy(
            gath.at[me], gath.at[me], ag_s.at[k], ag_r.at[k],
            device_id={"ctx": peer}, device_id_type=MESH)

    def take_sum(k):
        peer = lax.rem(me + devices - k, devices)
        return pltpu.make_async_remote_copy(
            gath.at[peer], gath.at[peer], ag_s.at[k], ag_r.at[k],
            device_id={"ctx": lax.rem(me + k, devices)}, device_id_type=MESH)

    for c in range(chunks):
        send_inc(c).start()

    loads[1].wait()
    loads[2].wait()
    for c in range(chunks):
        z = qkv[1, :, cols(c)].astype(F32) * qkv[2, :, cols(c)].astype(F32)
        zz[pl.ds(0, count), cols(c)] = z.astype(BF16)

        @pl.when(jnp.logical_not(last))
        def _():
            send_z(c).start()

    @pl.when(first)
    def _():
        zz[pl.ds(count, count), :] = jnp.zeros((count, channels), BF16)

    @pl.when(last)
    def _():
        gg[pl.ds(count, count), :] = jnp.zeros((count, channels), BF16)
        dsc[:, pl.ds(count, RIM), :] = jnp.zeros((3, RIM, channels), F32)

    square = (count, count)
    down = lax.broadcasted_iota(jnp.int32, square, 0)
    across = lax.broadcasted_iota(jnp.int32, square, 1)
    base = me * count

    def one(flag):
        return jnp.where(flag, 1.0, 0.0).astype(F32)

    pos_down = positions(base + down, docs_ref)
    lag = down - across
    m_own[...] = one((lag >= 0) & (lag <= pos_down)).astype(BF16)
    m_prev[...] = one((lag < 0) & (lag + count <= pos_down)).astype(BF16)
    turned = count - 1 - down
    pos_turned = positions(base + turned, docs_ref)
    lag = turned - across
    r_own[...] = one((lag >= 0) & (lag <= pos_turned))
    r_prev[...] = one((lag < 0) & (lag + count <= pos_turned))
    line = lax.broadcasted_iota(jnp.int32, (8, count), 1)
    pos_line = positions(base + line, docs_ref)[0:1]
    pos_ahead = positions(base + count + line, docs_ref)[0:1]
    lag = across - down
    t_own[...] = one((lag >= 0) & (lag <= pos_line)).astype(BF16)
    more = jnp.where(last, 0, 1)
    t_next[...] = one((lag < 0) & (lag + count <= pos_ahead) & (more > 0)).astype(BF16)
    for j in range(1, u_rows.shape[0] + 1):
        rows = base + down[:, :LANES] + j
        u_rows[j - 1] = one((j <= positions(rows, docs_ref)) & (rows < devices * count))
    straight = one(down == across).astype(BF16)
    lapped = one((down + across == 0) | (down + across == count)).astype(BF16)
    flip = one(down + across == count - 1)
    sides = (((0,), (0,)), ((), ()))
    filt = filt_ref[0]
    fdir[...] = lax.dot_general(filt, straight, sides, preferred_element_type=F32)
    frev[...] = lax.dot_general(filt, lapped, sides, preferred_element_type=F32)
    shortf[...] = short_ref[0].astype(F32)
    lane_group = lax.broadcasted_iota(jnp.int32, (count, LANES), 1) // members

    def toeplitz(source, tile, near, far):
        block = source[pl.ds(pl.multiple_of(tile * per_tile, per_tile), per_tile), :]
        for g in range(per_tile):
            full = jnp.broadcast_to(block[g:g + 1], square)
            ring = pltpu.roll(full, 0, 1, stride=1, stride_axis=0).astype(BF16)
            lhs[g * count:(g + 1) * count, :count] = ring * near[...]
            lhs[g * count:(g + 1) * count, count:] = ring * far[...]

    def picked(product):
        total = product[:count]
        for g in range(1, per_tile):
            total = jnp.where(lane_group == g, product[g * count:(g + 1) * count], total)
        return total

    def lanes(tile):
        return pl.ds(pl.multiple_of(tile * LANES, LANES), LANES)

    for c in range(chunks):
        @pl.when(jnp.logical_not(first))
        def _():
            send_z(c).wait_recv()

        def forward(i, carry):
            tile = c * tiles + i
            toeplitz(frev, tile, m_own, m_prev)
            product = jnp.dot(lhs[...], zz[:, lanes(tile)], preferred_element_type=F32)
            ysc[:, lanes(tile)] = picked(product)
            return carry

        lax.fori_loop(0, tiles, forward, 0)

    loads[0].wait()
    for c in range(chunks):
        send_inc(c).wait_recv()
        wide_inc = inc[:, cols(c)].astype(F32)
        gg[pl.ds(0, count), cols(c)] = (wide_inc * qkv[0, :, cols(c)].astype(F32)).astype(BF16)

        @pl.when(jnp.logical_not(first))
        def _():
            send_g(c).start()

        dsc[0, pl.ds(0, count), cols(c)] = (wide_inc * ysc[:, cols(c)]).astype(BF16).astype(F32)

        def pairs(i, carry):
            tile = c * tiles + i
            own = gg[pl.ds(0, count), lanes(tile)]
            back = jnp.dot(flip.astype(BF16), own, preferred_element_type=F32)
            for g in range(per_tile):
                lhs3[g * count:(g + 1) * count, :] = jnp.where(
                    lane_group == g, back, 0.0).astype(BF16)
            product = lax.dot_general(
                lhs3[...], zz[:, lanes(tile)], (((1,), (1,)), ((), ())),
                preferred_element_type=F32)
            sums = []
            for g in range(per_tile):
                near = product[g * count:(g + 1) * count, :count]
                far = product[g * count:(g + 1) * count, count:]
                both = near * r_own[...] + far * r_prev[...]
                slid = pltpu.roll(both, 0, 1, stride=1, stride_axis=0)
                sums.append(jnp.sum(slid, axis=0, keepdims=True))
            acc[pl.ds(pl.multiple_of(tile * per_tile, per_tile), per_tile), :] = (
                jnp.concatenate(sums, axis=0))
            return carry

        lax.fori_loop(0, tiles, pairs, 0)

    for d in range(devices):
        part[d] = acc[d * share:(d + 1) * share, :]

    def start_part(k, carry):
        send_part(k).start()
        return carry

    lax.fori_loop(1, devices, start_part, 0)

    for c in range(chunks):
        @pl.when(jnp.logical_not(last))
        def _():
            send_g(c).wait_recv()

        def backward(i, carry):
            tile = c * tiles + i
            toeplitz(fdir, tile, t_own, t_next)
            product = jnp.dot(lhs[...], gg[:, lanes(tile)], preferred_element_type=F32)
            mixed = picked(product)
            key = qkv[1, :, lanes(tile)].astype(F32)
            value = qkv[2, :, lanes(tile)].astype(F32)
            dsc[1, pl.ds(0, count), lanes(tile)] = (mixed * value).astype(BF16).astype(F32)
            dsc[2, pl.ds(0, count), lanes(tile)] = (mixed * key).astype(BF16).astype(F32)
            return carry

        lax.fori_loop(0, tiles, backward, 0)

        @pl.when(jnp.logical_not(first))
        def _():
            send_rim(c).start()

    def land_part(k, total):
        send_part(k).wait_recv()
        return total + parts_in[k]

    gath[me] = lax.fori_loop(1, devices, land_part, part[me])

    def start_sum(k, carry):
        send_sum(k).start()
        return carry

    lax.fori_loop(1, devices, start_sum, 0)

    def store(c):
        return pltpu.make_async_copy(
            obuf.at[:, :, cols(c)], out_hbm.at[0, :, :, cols(c)], out_sem.at[c])

    for c in range(chunks):
        @pl.when(jnp.logical_not(last))
        def _():
            send_rim(c).wait_recv()

        def short(i, carry):
            tile = c * tiles + i
            for s in range(3):
                total = dsc[s, pl.ds(0, count), lanes(tile)] * shortf[s, pl.ds(0, 1), lanes(tile)]
                for j in range(1, u_rows.shape[0] + 1):
                    moved = dsc[s, pl.ds(j, count), lanes(tile)]
                    weight = shortf[s, pl.ds(j, 1), lanes(tile)]
                    total = total + (moved * weight) * u_rows[j - 1]
                obuf[s, :, lanes(tile)] = total.astype(BF16)
            return carry

        lax.fori_loop(0, tiles, short, 0)
        store(c).start()

    def land_sum(k, carry):
        take_sum(k).wait_recv()
        return carry

    lax.fori_loop(1, devices, land_sum, 0)
    for d in range(devices):
        acc[d * share:(d + 1) * share, :] = gath[d]
    summed = lax.dot_general(
        flip, acc[...], (((1,), (1,)), ((), ())),
        preferred_element_type=F32, precision=lax.Precision.HIGHEST)
    fg_ref[0] = summed / math.sqrt(count * devices * members)

    def left(k, carry):
        send_part(k).wait_send()
        send_sum(k).wait_send()
        return carry

    lax.fori_loop(1, devices, left, 0)
    for c in range(chunks):
        send_inc(c).wait_send()
        store(c).wait()

        @pl.when(jnp.logical_not(last))
        def _():
            send_z(c).wait_send()

        @pl.when(jnp.logical_not(first))
        def _():
            send_g(c).wait_send()
            send_rim(c).wait_send()


def body(sections, devices, saved_qkv, handed, long_filter, short_filter, doc_lengths):
    _, _, count, channels = saved_qkv.shape
    _, taps, groups = long_filter.shape
    short_taps = short_filter.shape[2]
    assert taps == count and groups % devices == 0
    chunks = max(1, math.gcd(channels // LANES, 4))
    per_tile = LANES // (channels // groups)
    share = groups // devices
    dma = pltpu.SemaphoreType.DMA
    vmem = pltpu.VMEM
    hbm = pl.BlockSpec(memory_space=pl.ANY)
    local = pl.BlockSpec(memory_space=pltpu.VMEM)
    return pl.pallas_call(
        functools.partial(kernel, sections, devices, chunks),
        out_shape=(
            jax.ShapeDtypeStruct(saved_qkv.shape, BF16),
            jax.ShapeDtypeStruct(long_filter.shape, F32),
        ),
        in_specs=[pl.BlockSpec(memory_space=pltpu.SMEM), hbm, hbm, local, local],
        out_specs=(hbm, local),
        scratch_shapes=[
            vmem((3, count, channels), BF16),
            vmem((count, channels), BF16),
            vmem((2 * count, channels), BF16),
            vmem((2 * count, channels), BF16),
            vmem((count, channels), F32),
            vmem((3, count + RIM, channels), F32),
            vmem((3, count, channels), BF16),
            vmem((per_tile * count, 2 * count), BF16),
            vmem((per_tile * count, LANES), BF16),
            vmem((groups, count), F32),
            vmem((groups, count), F32),
            vmem((3, short_taps, channels), F32),
            vmem((count, count), BF16),
            vmem((count, count), BF16),
            vmem((count, count), BF16),
            vmem((count, count), BF16),
            vmem((count, count), F32),
            vmem((count, count), F32),
            vmem((short_taps - 1, count, LANES), F32),
            vmem((groups, count), F32),
            vmem((devices, share, count), F32),
            vmem((devices, share, count), F32),
            vmem((devices, share, count), F32),
            dma((3,)), dma((chunks,)),
            dma((chunks,)), dma((chunks,)),
            dma((chunks,)), dma((chunks,)),
            dma((chunks,)), dma((chunks,)),
            dma((chunks,)), dma((chunks,)),
            dma((devices,)), dma((devices,)),
            dma((devices,)), dma((devices,)),
        ],
        compiler_params=pltpu.CompilerParams(collective_id=0, has_side_effects=True),
    )(doc_lengths, saved_qkv, handed, long_filter, short_filter)


def solution(mesh):
    return jax.shard_map(
        functools.partial(body, mesh.shape["pipe"], mesh.shape["ctx"]),
        mesh=mesh,
        in_specs=(
            P("pipe", None, "ctx", None),
            P("pipe", "ctx", None),
            P("pipe", None, None),
            P("pipe", None, None, None),
            P(),
        ),
        out_specs=(P("pipe", None, "ctx", None), P("pipe", None, None)),
        check_vma=False,
    )
```

time: 411 us -> 41.5 us (0.10)
  other arithmetic: 200 us -> 0 us
  waiting for transfers between devices: 110 us -> 0 us
  local copies, waits for them, and re-layouts: 61.2 us -> 3.39 us
  Pallas kernels: 0 us -> 37.3 us
  loops' own time: 14.2 us -> 0 us
  between operations: 14.3 us -> 0.65 us
  starting transfers between devices: 9.33 us -> 0 us
    add x17 -> x0, other arithmetic: 122 us -> none  [the longest x8 76.8 us: forward_step(): total = total + jnp.where(usable, shifted * weights[None, :], 0.0)]
    psum x1 -> x0, waiting for transfers between devices: 82.1 us -> none  [body(): summed = lax.psum(filter_sum, 'ctx')]
    reduce_sum x72 -> x0, other arithmetic: 62.8 us -> none  [the longest x8 55.5 us: forward_step(): jnp.sum((grad_wide * shifted).reshape(row_count, groups, members), axis=2)]
    pallas_call x0 -> x1, Pallas kernels: none -> 37.3 us  [body(): pl.pallas_call(functools.partial(kernel, sections, devices, chunks), out_...]
    ppermute x4 -> x0, waiting for transfers between devices: 27.8 us -> none  [the longest x3 16 us: shifted_2(): return lax.ppermute(block, axis, route)]
    mul x256 -> x0, local copies, waits for them, and re-layouts: 24.4 us -> none  [the longest x128 12.2 us: forward_step(): total = total + jnp.where(usable, shifted * weights[None, :], 0.0)]
    broadcast_in_dim x256 -> x0, local copies, waits for them, and re-layouts: 18.6 us -> none  [the longest x128 9.31 us: step(): weights = jnp.repeat(filt[lag].astype(jnp.float32), members)]
    another operation x2 -> x0, loops' own time: 14.2 us -> none  [the longest x1 7.35 us: back_conv(): lax.scan(step, jnp.zeros((out_len, channels), jnp.float32), bases)]
  transfers between devices with their start and end apart: 5 -> 0, of which waited for: 5 -> 0; matrix products, arithmetic and copies ran while one was open for 1% -> 0% of each run, Pallas kernels for 0% -> 0%
where the time goes in v1:
time: 41.5 us; the launch traced here: 41.3 us
  Pallas kernels  37.3 us (90%)
  local copies, waits for them, and re-layouts  3.39 us (8%)
  between operations  0.65 us (2%)
    pallas_call x1, Pallas kernels, body(): pl.pallas_call(functools.partial(kernel, sections, devices, chunks), out_...  37.3 us
    unnamed x4, local copies, waits for them, and re-layouts  3.39 us

profile of v1, /device:TPU:1, one launch (start us, length us, event | category | flops | bytes accessed | tf_op | source)
XLA Modules:
  0.0 41.3 jit_solution(12022539434833705170)
XLA Ops:
  0.6 37.3 %shard_map.68 = (bf16[1,3,128,2048]{3,2,1,0:T(8,128)(2,1)}, f32[1,128,128]{2,1,0:T(8,128)}) custom-call(s32[16]{0:T(128)} %docs_ref.1, bf16[1,3,128,2048]{3,2,1,0:T(8,128)(2,1)} %qkv_hbm.1, bf16[1,128,2048]{2,1,0:T(8,128)(2,1)} %handed_hbm.1, bf16[1,128,128]{2,1,0:T(8,128)(2,1)} %filt_ref.1, bf16[1,3,3,2048]{3,2,1,0:T(4,128)(2,1)} %short_ref.1), custom_call_target="tpu_custom_call" | custom-call | tf_op jit(solution)/shard_map/pallas_call | solution.py:345
  37.9 0.0 copy-start
  37.9 2.8 %copy.9 = bf16[1,3,128,2048]{3,2,1,0:T(8,128)(2,1)} copy(bf16[1,3,128,2048]{3,2,1,0:T(8,128)(2,1)} %get-tuple-element.4) | data formatting | bytes 3145728
  40.7 0.0 copy-done
  40.7 0.6 %copy.10 = f32[1,128,128]{2,1,0:T(8,128)} copy(f32[1,128,128]{2,1,0:T(8,128)S(1)} %copy-done) | data formatting | bytes 131072
Async XLA Ops:
  37.9 2.8 %copy-start = (f32[1,128,128]{2,1,0:T(8,128)S(1)}, f32[1,128,128]{2,1,0:T(8,128)}, u32[]{:S(2)}) copy-start(f32[1,128,128]{2,1,0:T(8,128)} %get-tuple-element.5) | copy-start | bytes 196612

commit v2 on v1

--- a/solution.py
+++ b/solution.py
@@ -197,6 +197,51 @@
 
         lax.fori_loop(0, tiles, forward, 0)
 
+    def backward_chunk(c):
+        @pl.when(jnp.logical_not(last))
+        def _():
+            send_g(c).wait_recv()
+
+        def backward(i, carry):
+            tile = c * tiles + i
+            toeplitz(fdir, tile, t_own, t_next)
+            product = jnp.dot(lhs[...], gg[:, lanes(tile)], preferred_element_type=F32)
+            mixed = picked(product)
+            key = qkv[1, :, lanes(tile)].astype(F32)
+            value = qkv[2, :, lanes(tile)].astype(F32)
+            dsc[1, pl.ds(0, count), lanes(tile)] = (mixed * value).astype(BF16).astype(F32)
+            dsc[2, pl.ds(0, count), lanes(tile)] = (mixed * key).astype(BF16).astype(F32)
+            return carry
+
+        lax.fori_loop(0, tiles, backward, 0)
+
+        @pl.when(jnp.logical_not(first))
+        def _():
+            send_rim(c).start()
+
+    def store(c):
+        return pltpu.make_async_copy(
+            obuf.at[:, :, cols(c)], out_hbm.at[0, :, :, cols(c)], out_sem.at[c])
+
+    def short_chunk(c):
+        @pl.when(jnp.logical_not(last))
+        def _():
+            send_rim(c).wait_recv()
+
+        def short(i, carry):
+            tile = c * tiles + i
+            for s in range(3):
+                total = dsc[s, pl.ds(0, count), lanes(tile)] * shortf[s, pl.ds(0, 1), lanes(tile)]
+                for j in range(1, u_rows.shape[0] + 1):
+                    moved = dsc[s, pl.ds(j, count), lanes(tile)]
+                    weight = shortf[s, pl.ds(j, 1), lanes(tile)]
+                    total = total + (moved * weight) * u_rows[j - 1]
+                obuf[s, :, lanes(tile)] = total.astype(BF16)
+            return carry
+
+        lax.fori_loop(0, tiles, short, 0)
+        store(c).start()
+
     loads[0].wait()
     for c in range(chunks):
         send_inc(c).wait_recv()
@@ -231,6 +276,8 @@
             return carry
 
         lax.fori_loop(0, tiles, pairs, 0)
+        if c >= 2:
+            backward_chunk(c - 2)
 
     for d in range(devices):
         part[d] = acc[d * share:(d + 1) * share, :]
@@ -241,27 +288,11 @@
 
     lax.fori_loop(1, devices, start_part, 0)
 
-    for c in range(chunks):
-        @pl.when(jnp.logical_not(last))
-        def _():
-            send_g(c).wait_recv()
-
-        def backward(i, carry):
-            tile = c * tiles + i
-            toeplitz(fdir, tile, t_own, t_next)
-            product = jnp.dot(lhs[...], gg[:, lanes(tile)], preferred_element_type=F32)
-            mixed = picked(product)
-            key = qkv[1, :, lanes(tile)].astype(F32)
-            value = qkv[2, :, lanes(tile)].astype(F32)
-            dsc[1, pl.ds(0, count), lanes(tile)] = (mixed * value).astype(BF16).astype(F32)
-            dsc[2, pl.ds(0, count), lanes(tile)] = (mixed * key).astype(BF16).astype(F32)
-            return carry
-
-        lax.fori_loop(0, tiles, backward, 0)
-
-        @pl.when(jnp.logical_not(first))
-        def _():
-            send_rim(c).start()
+    for c in range(max(chunks - 2, 0), chunks):
+        backward_chunk(c)
+    held = max(chunks - 2, 0)
+    for c in range(held):
+        short_chunk(c)
 
     def land_part(k, total):
         send_part(k).wait_recv()
@@ -275,28 +306,8 @@
 
     lax.fori_loop(1, devices, start_sum, 0)
 
-    def store(c):
-        return pltpu.make_async_copy(
-            obuf.at[:, :, cols(c)], out_hbm.at[0, :, :, cols(c)], out_sem.at[c])
-
-    for c in range(chunks):
-        @pl.when(jnp.logical_not(last))
-        def _():
-            send_rim(c).wait_recv()
-
-        def short(i, carry):
-            tile = c * tiles + i
-            for s in range(3):
-                total = dsc[s, pl.ds(0, count), lanes(tile)] * shortf[s, pl.ds(0, 1), lanes(tile)]
-                for j in range(1, u_rows.shape[0] + 1):
-                    moved = dsc[s, pl.ds(j, count), lanes(tile)]
-                    weight = shortf[s, pl.ds(j, 1), lanes(tile)]
-                    total = total + (moved * weight) * u_rows[j - 1]
-                obuf[s, :, lanes(tile)] = total.astype(BF16)
-            return carry
-
-        lax.fori_loop(0, tiles, short, 0)
-        store(c).start()
+    for c in range(held, chunks):
+        short_chunk(c)
 
     def land_sum(k, carry):
         take_sum(k).wait_recv()
@@ -335,7 +346,7 @@
     _, taps, groups = long_filter.shape
     short_taps = short_filter.shape[2]
     assert taps == count and groups % devices == 0
-    chunks = max(1, math.gcd(channels // LANES, 4))
+    chunks = max(1, math.gcd(channels // LANES, 8))
     per_tile = LANES // (channels // groups)
     share = groups // devices
     dma = pltpu.SemaphoreType.DMA

time: 41.5 us -> 44 us (1.060)
  Pallas kernels: 37.3 us -> 39.4 us
    pallas_call x1, Pallas kernels: 37.3 us -> 39.4 us  [body(): pl.pallas_call(functools.partial(kernel, sections, devices, chunks), out_...]
where the time goes in v2:
time: 44 us; the launch traced here: 43.4 us
  Pallas kernels  39.4 us (90%)
  local copies, waits for them, and re-layouts  3.39 us (8%)
  between operations  0.65 us (1%)
    pallas_call x1, Pallas kernels, body(): pl.pallas_call(functools.partial(kernel, sections, devices, chunks), out_...  39.4 us
    unnamed x4, local copies, waits for them, and re-layouts  3.39 us

profile of v2, /device:TPU:1, one launch (start us, length us, event | category | flops | bytes accessed | tf_op | source)
XLA Modules:
  0.0 43.4 jit_solution(14713515106474445218)
XLA Ops:
  0.6 39.4 %shard_map.68 = (bf16[1,3,128,2048]{3,2,1,0:T(8,128)(2,1)}, f32[1,128,128]{2,1,0:T(8,128)}) custom-call(s32[16]{0:T(128)} %docs_ref.1, bf16[1,3,128,2048]{3,2,1,0:T(8,128)(2,1)} %qkv_hbm.1, bf16[1,128,2048]{2,1,0:T(8,128)(2,1)} %handed_hbm.1, bf16[1,128,128]{2,1,0:T(8,128)(2,1)} %filt_ref.1, bf16[1,3,3,2048]{3,2,1,0:T(4,128)(2,1)} %short_ref.1), custom_call_target="tpu_custom_call" | custom-call | tf_op jit(solution)/shard_map/pallas_call | solution.py:356
  40.0 0.0 copy-start
  40.0 2.8 %copy.9 = bf16[1,3,128,2048]{3,2,1,0:T(8,128)(2,1)} copy(bf16[1,3,128,2048]{3,2,1,0:T(8,128)(2,1)} %get-tuple-element.4) | data formatting | bytes 3145728
  42.8 0.0 copy-done
  42.8 0.6 %copy.10 = f32[1,128,128]{2,1,0:T(8,128)} copy(f32[1,128,128]{2,1,0:T(8,128)S(1)} %copy-done) | data formatting | bytes 131072
Async XLA Ops:
  40.0 2.8 %copy-start = (f32[1,128,128]{2,1,0:T(8,128)S(1)}, f32[1,128,128]{2,1,0:T(8,128)}, u32[]{:S(2)}) copy-start(f32[1,128,128]{2,1,0:T(8,128)} %get-tuple-element.5) | copy-start | bytes 196612

commit v3 on v1

--- a/solution.py
+++ b/solution.py
@@ -31,7 +31,7 @@
     qkv, inc, zz, gg, ysc, dsc, obuf, lhs, lhs3, fdir, frev, shortf,
     m_own, m_prev, t_own, t_next, r_own, r_prev, u_rows,
     acc, part, parts_in, gath,
-    in_sem, out_sem, inc_s, inc_r, z_s, z_r, g_s, g_r, rim_s, rim_r, rs_s, rs_r, ag_s, ag_r,
+    in_sem, out_sem, inc_s, inc_r, z_s, z_r, g_s, g_r, rim_s, rim_r, rs_s, rs_r, ag_s, ag_r, ready,
 ):
     sec = lax.axis_index("pipe")
     me = lax.axis_index("ctx")
@@ -55,13 +55,25 @@
     barrier = pltpu.get_barrier_semaphore()
     pl.semaphore_signal(barrier, inc=1, device_id={"pipe": behind}, device_id_type=MESH)
 
-    def greet(k, carry):
-        peer = lax.rem(me + k, devices)
+    for step in (1, devices - 1):
+        peer = lax.rem(me + step, devices)
         pl.semaphore_signal(barrier, inc=1, device_id={"ctx": peer}, device_id_type=MESH)
-        return carry
-
-    lax.fori_loop(1, devices, greet, 0)
-    pl.semaphore_wait(barrier, devices)
+    pl.semaphore_wait(barrier, 3)
+
+    reaches = []
+    while 2 ** len(reaches) < devices // 2:
+        reaches.append(2 ** len(reaches))
+
+    def tell(r):
+        if r < len(reaches):
+            for step in (reaches[r], devices - reaches[r]):
+                peer = lax.rem(me + step, devices)
+                pl.semaphore_signal(
+                    ready.at[r], inc=1, device_id={"ctx": peer}, device_id_type=MESH)
+
+    def hear(r):
+        if r < len(reaches):
+            pl.semaphore_wait(ready.at[r], 2)
 
     def cols(c):
         return pl.ds(c * wide, wide)
@@ -109,6 +121,7 @@
 
     for c in range(chunks):
         send_inc(c).start()
+    tell(0)
 
     loads[1].wait()
     loads[2].wait()
@@ -196,6 +209,8 @@
             return carry
 
         lax.fori_loop(0, tiles, forward, 0)
+        hear(c)
+        tell(c + 1)
 
     loads[0].wait()
     for c in range(chunks):
@@ -232,6 +247,9 @@
 
         lax.fori_loop(0, tiles, pairs, 0)
 
+    for r in range(chunks, len(reaches)):
+        hear(r)
+        tell(r + 1)
     for d in range(devices):
         part[d] = acc[d * share:(d + 1) * share, :]
 
@@ -381,6 +399,7 @@
             dma((chunks,)), dma((chunks,)),
             dma((devices,)), dma((devices,)),
             dma((devices,)), dma((devices,)),
+            pltpu.SemaphoreType.REGULAR((max(1, devices.bit_length()),)),
         ],
         compiler_params=pltpu.CompilerParams(collective_id=0, has_side_effects=True),
     )(doc_lengths, saved_qkv, handed, long_filter, short_filter)

time: 41.5 us -> 41.7 us (level); the launches traced: 41.3 us -> 41.1 us
  no operation moved by 1% of the time
where the time goes in v3:
time: 41.7 us; the launch traced here: 41.1 us
  Pallas kernels  37 us (89%)
  local copies, waits for them, and re-layouts  3.39 us (8%)
  between operations  0.65 us (2%)
    pallas_call x1, Pallas kernels, body(): pl.pallas_call(functools.partial(kernel, sections, devices, chunks), out_...  37 us
    unnamed x4, local copies, waits for them, and re-layouts  3.39 us

profile of v3, /device:TPU:1, one launch (start us, length us, event | category | flops | bytes accessed | tf_op | source)
XLA Modules:
  0.0 41.1 jit_solution(9131075388529884494)
XLA Ops:
  0.6 37.0 %shard_map.68 = (bf16[1,3,128,2048]{3,2,1,0:T(8,128)(2,1)}, f32[1,128,128]{2,1,0:T(8,128)}) custom-call(s32[16]{0:T(128)} %docs_ref.1, bf16[1,3,128,2048]{3,2,1,0:T(8,128)(2,1)} %qkv_hbm.1, bf16[1,128,2048]{2,1,0:T(8,128)(2,1)} %handed_hbm.1, bf16[1,128,128]{2,1,0:T(8,128)(2,1)} %filt_ref.1, bf16[1,3,3,2048]{3,2,1,0:T(4,128)(2,1)} %short_ref.1), custom_call_target="tpu_custom_call" | custom-call | tf_op jit(solution)/shard_map/pallas_call | solution.py:363
  37.7 0.0 copy-start
  37.7 2.8 %copy.9 = bf16[1,3,128,2048]{3,2,1,0:T(8,128)(2,1)} copy(bf16[1,3,128,2048]{3,2,1,0:T(8,128)(2,1)} %get-tuple-element.4) | data formatting | bytes 3145728
  40.4 0.0 copy-done
  40.4 0.6 %copy.10 = f32[1,128,128]{2,1,0:T(8,128)} copy(f32[1,128,128]{2,1,0:T(8,128)S(1)} %copy-done) | data formatting | bytes 131072
Async XLA Ops:
  37.7 2.8 %copy-start = (f32[1,128,128]{2,1,0:T(8,128)S(1)}, f32[1,128,128]{2,1,0:T(8,128)}, u32[]{:S(2)}) copy-start(f32[1,128,128]{2,1,0:T(8,128)} %get-tuple-element.5) | copy-start | bytes 196612

commit v4 on v3

--- a/solution.py
+++ b/solution.py
@@ -259,6 +259,15 @@
 
     lax.fori_loop(1, devices, start_part, 0)
 
+    def land_part(k, total):
+        send_part(k).wait_recv()
+        return total + parts_in[k]
+
+
+    def start_sum(k, carry):
+        send_sum(k).start()
+        return carry
+
     for c in range(chunks):
         @pl.when(jnp.logical_not(last))
         def _():
@@ -281,17 +290,9 @@
         def _():
             send_rim(c).start()
 
-    def land_part(k, total):
-        send_part(k).wait_recv()
-        return total + parts_in[k]
-
-    gath[me] = lax.fori_loop(1, devices, land_part, part[me])
-
-    def start_sum(k, carry):
-        send_sum(k).start()
-        return carry
-
-    lax.fori_loop(1, devices, start_sum, 0)
+        if c == max(chunks - 2, 0):
+            gath[me] = lax.fori_loop(1, devices, land_part, part[me])
+            lax.fori_loop(1, devices, start_sum, 0)
 
     def store(c):
         return pltpu.make_async_copy(

time: 41.7 us -> 40.5 us (0.971)
  Pallas kernels: 37 us -> 36.2 us
    pallas_call x1, Pallas kernels: 37 us -> 36.2 us  [body(): pl.pallas_call(functools.partial(kernel, sections, devices, chunks), out_...]
where the time goes in v4:
time: 40.5 us; the launch traced here: 40.3 us
  Pallas kernels  36.2 us (89%)
  local copies, waits for them, and re-layouts  3.39 us (8%)
  between operations  0.65 us (2%)
    pallas_call x1, Pallas kernels, body(): pl.pallas_call(functools.partial(kernel, sections, devices, chunks), out_...  36.2 us
    unnamed x4, local copies, waits for them, and re-layouts  3.39 us

profile of v4, /device:TPU:1, one launch (start us, length us, event | category | flops | bytes accessed | tf_op | source)
XLA Modules:
  0.0 40.3 jit_solution(8700051101901743990)
XLA Ops:
  0.6 36.2 %shard_map.68 = (bf16[1,3,128,2048]{3,2,1,0:T(8,128)(2,1)}, f32[1,128,128]{2,1,0:T(8,128)}) custom-call(s32[16]{0:T(128)} %docs_ref.1, bf16[1,3,128,2048]{3,2,1,0:T(8,128)(2,1)} %qkv_hbm.1, bf16[1,128,2048]{2,1,0:T(8,128)(2,1)} %handed_hbm.1, bf16[1,128,128]{2,1,0:T(8,128)(2,1)} %filt_ref.1, bf16[1,3,3,2048]{3,2,1,0:T(4,128)(2,1)} %short_ref.1), custom_call_target="tpu_custom_call" | custom-call | tf_op jit(solution)/shard_map/pallas_call | solution.py:364
  36.9 0.0 copy-start
  36.9 2.8 %copy.9 = bf16[1,3,128,2048]{3,2,1,0:T(8,128)(2,1)} copy(bf16[1,3,128,2048]{3,2,1,0:T(8,128)(2,1)} %get-tuple-element.4) | data formatting | bytes 3145728
  39.6 0.0 copy-done
  39.7 0.6 %copy.10 = f32[1,128,128]{2,1,0:T(8,128)} copy(f32[1,128,128]{2,1,0:T(8,128)S(1)} %copy-done) | data formatting | bytes 131072
Async XLA Ops:
  36.9 2.8 %copy-start = (f32[1,128,128]{2,1,0:T(8,128)S(1)}, f32[1,128,128]{2,1,0:T(8,128)}, u32[]{:S(2)}) copy-start(f32[1,128,128]{2,1,0:T(8,128)} %get-tuple-element.5) | copy-start | bytes 196612
